TPU v7x, 32 devices: a whole 2x2x4 slice. The times are simulated.
32 devices in a mesh: section: 4 (over y, x), dom: 8 (over z, core).
Axes of the slice: x: 2, y: 2, z: 4, core: 2. Of those that a mesh axis runs over, the one named last changes fastest.
Arguments:
- stacked: bfloat16 [4, 1024, 1024], P('section', 'dom'), may hold values from -6 to 6
- edges: int32 [1024, 256], P('dom'), may hold values 0 or 1
- picks: int32 [16, 3], P('dom'), may hold values from 0 to 2
- self_w: bfloat16 [4, 1024, 1024], P('section'), may hold values from -0.1875 to 0.1875
- neigh_w: bfloat16 [4, 1024, 1024], P('section'), may hold values from -0.75 to 0.75
Outputs:
- embeddings: bfloat16 [4, 1024, 1024], P('section', 'dom')
Inputs may be any that keep to these rules, and one draw needn't show every extreme that they name: `picks`: A value of 2 means that the destination block has no tile from that direction; smaller values name a slab of the peer partition.
All inputs are finite; a program needn't handle non-finite values. No bound on the sum of `edges` on one device may be relied on, other than what follows from the above.
Results may differ from a plain program's by a relative error of at most 0.006.
Values may be sent and summed in bfloat16 or wider, within the bound.
A program may use at most 64 MiB of HBM per device.

v0:
```python
import functools

import jax
import jax.numpy as jnp
from jax import lax
from jax.experimental import pallas as pl
from jax.experimental.pallas import tpu as pltpu
from jax.sharding import PartitionSpec as P

PEER_OFFSETS = (-1, 1, 2)
MESH = pl.DeviceIdType.MESH


def kernel(
    ns, nd, slabs, nch,
    stacked, edges, picks, ws_hbm, wn_hbm, out,
    ws, wn, src, masks, pre, acc, stage, above, sums, summed_below,
    wsem, zsend, zrecv, xsend, xrecv, psend, precv,
):
    block = edges.shape[1] // (len(PEER_OFFSETS) + 1)
    width = stacked.shape[1]
    cw = width // nch
    s = lax.axis_index("section")
    p = lax.axis_index("dom")

    def at(section, dom):
        return {"section": section, "dom": dom}

    w_self = pltpu.make_async_copy(ws_hbm, ws, wsem.at[0])
    w_neigh = pltpu.make_async_copy(wn_hbm, wn, wsem.at[1])
    w_self.start()
    w_neigh.start()

    barrier = pltpu.get_barrier_semaphore()
    greeted = [at(s, lax.rem(p + o + nd, nd)) for o in (-2, -1, 1, 2)]
    greeted += [at(lax.rem(s + 1, ns), p), at(lax.rem(s + ns - 1, ns), p)]
    for device in greeted:
        pl.semaphore_signal(barrier, inc=1, device_id=device, device_id_type=MESH)

    def rows(c):
        return pl.ds(c * block, block)

    def cols(ch):
        return pl.ds(ch * cw, cw)

    last = slabs - 1

    even = lax.rem(p, 2) == 0
    partner = p + 1 - 2 * lax.rem(p, 2)
    far = len(PEER_OFFSETS) - 1

    def z_copy(src_ref, slot, ch, k):
        return pltpu.make_async_remote_copy(
            src_ref=src_ref,
            dst_ref=src.at[slot, rows(k + 1), cols(ch)],
            send_sem=zsend.at[slot, ch, k],
            recv_sem=zrecv.at[slot, ch, k],
            device_id=at(s, partner if k == 1 else lax.rem(p - PEER_OFFSETS[k] + nd, nd)),
            device_id_type=MESH,
        )

    def z_send(src_ref, slot, ch):
        z_copy(src_ref, slot, ch, 0).start()
        z_copy(src_ref, slot, ch, 2).start()

        @pl.when(jnp.logical_not(even))
        def _():
            z_copy(src_ref, slot, ch, 1).start()

    def relay(slot, ch):
        z_copy(own(slot, ch), slot, ch, 2).wait_recv()

        @pl.when(even)
        def _():
            z_copy(src.at[slot, rows(far + 1), cols(ch)], slot, ch, 1).start()

    def z_wait(slot, ch):
        for k in (0, 1):
            z_copy(own(slot, ch), slot, ch, k).wait_recv()

    def x_copy(c, ch):
        return pltpu.make_async_remote_copy(
            src_ref=stage.at[c, :, cols(ch)],
            dst_ref=src.at[0, rows(0), cols(ch)] if c == 0 else above.at[c - 1, :, cols(ch)],
            send_sem=xsend.at[c, ch],
            recv_sem=xrecv.at[c, ch],
            device_id=at(lax.rem(s + 1, ns), p),
            device_id_type=MESH,
        )

    def sum_copy(c, ch):
        return pltpu.make_async_remote_copy(
            src_ref=sums.at[c - 1, :, cols(ch)],
            dst_ref=summed_below.at[c - 1, :, cols(ch)],
            send_sem=psend.at[c - 1, ch],
            recv_sem=precv.at[c - 1, ch],
            device_id=at(lax.rem(s + 1, ns), p),
            device_id_type=MESH,
        )

    def given(j, ch):
        return stacked.at[rows(j), cols(ch)]

    def own(slot, ch):
        return src.at[slot, rows(0), cols(ch)]

    tile = lax.broadcasted_iota(jnp.int32, (block, edges.shape[1]), 1) // block
    degree = []
    for c in range(slabs):
        entries = edges[rows(c), :].astype(jnp.float32)
        total = jnp.ones((block, 1), jnp.float32)
        for j in range(slabs):
            scale = jnp.full(entries.shape, 1.0 if c == j else 0.0, jnp.float32)
            for k in range(len(PEER_OFFSETS)):
                wanted = jnp.where(picks[c, k] == j, 1.0, 0.0)
                scale = jnp.where(tile == k + 1, wanted, scale)
            masked = entries * scale
            masks[c, j] = masked.astype(jnp.bfloat16)
            total = total + jnp.sum(masked, axis=1, keepdims=True)
        degree.append(total)
    for j in range(1, slabs):
        src[j, rows(0), :] = stacked[rows(j), :]

    @pl.when(s == 0)
    def _():
        src[0, rows(0), :] = stacked[rows(0), :]

    pl.semaphore_wait(barrier, len(greeted))

    for ch in range(nch):
        @pl.when(s == 0)
        def _():
            z_send(given(0, ch), 0, ch)
        for j in range(1, slabs):
            z_send(given(j, ch), j, ch)

    def gather(c, j, slot, ch):
        return jnp.dot(
            masks[c, j], src[slot, :, cols(ch)], preferred_element_type=jnp.float32
        )

    def self_part(ref):
        for ch in range(nch):
            part = jnp.dot(
                ref[:, cols(ch)], ws[cols(ch), :], preferred_element_type=jnp.float32
            )
            if ch == 0:
                acc[...] = part
            else:
                acc[...] += part

    w_self.wait()

    @pl.when(s == 0)
    def _():
        self_part(src.at[0, rows(0)])

    for ch in range(nch):
        @pl.when(s == 0)
        def _():
            relay(0, ch)
        for j in range(1, slabs):
            relay(j, ch)

    w_neigh.wait()

    def produce(c, n, mean):
        hidden = acc[:, cols(n)] + jnp.dot(
            mean, wn[cols(nch - 1), cols(n)], preferred_element_type=jnp.float32
        )
        made = jnp.maximum(hidden, 0.0).astype(jnp.bfloat16)
        stage[c, :, cols(n)] = made
        out[rows(c), cols(n)] = made
        if c > 0:
            src[c + last, rows(0), cols(n)] = made

        @pl.when(s < ns - 1)
        def _():
            if c > 0:
                z_send(own(c + last, n), c + last, n)
            x_copy(c, n).start()

    def finish(c, ch, summed):
        mean = (summed / degree[c]).astype(jnp.bfloat16)
        if ch < nch - 1:
            acc[...] += jnp.dot(mean, wn[cols(ch), :], preferred_element_type=jnp.float32)
        else:
            for n in range(nch):
                produce(c, n, mean)

    @pl.when(s > 0)
    def _():
        for ch in range(nch):
            x_copy(0, ch).wait_recv()
            z_send(own(0, ch), 0, ch)
        self_part(src.at[0, rows(0)])

    for ch in range(nch):
        part = None
        for j in range(1, slabs):
            z_wait(j, ch)
            term = gather(0, j, j, ch)
            part = term if part is None else part + term
        pre[:, cols(ch)] = jnp.zeros((block, cw), jnp.float32) if part is None else part

    @pl.when(s > 0)
    def _():
        relay(0, 0)
    for ch in range(nch):
        z_wait(0, ch)
        if ch < nch - 1:
            @pl.when(s > 0)
            def _():
                relay(0, ch + 1)
        finish(0, ch, pre[:, cols(ch)] + gather(0, 0, 0, ch))

    for c in range(1, slabs):
        for ch in range(nch):
            part = gather(c, 0, 0, ch)
            for j in range(c + 1, slabs):
                part = part + gather(c, j, j, ch)
            pre[:, cols(ch)] = part

        @pl.when(s == 0)
        def _():
            self_part(src.at[c, rows(0)])
            for ch in range(nch):
                part = pre[:, cols(ch)]
                for j in range(1, c + 1):
                    part = part + gather(c, j, j, ch)
                pre[:, cols(ch)] = part

        @pl.when(s > 0)
        def _():
            for ch in range(nch):
                x_copy(c, ch).wait_recv()
            self_part(above.at[c - 1])

        for ch in range(nch):
            @pl.when(s > 0)
            def _():
                sum_copy(c, ch).wait_recv()
                pre[:, cols(ch)] += summed_below[c - 1, :, cols(ch)].astype(jnp.float32)
            finish(c, ch, pre[:, cols(ch)])

        @pl.when(s < ns - 1)
        def _():
            relay(c + last, 0)
            for ch in range(nch):
                if ch < nch - 1:
                    relay(c + last, ch + 1)
                z_wait(c + last, ch)
                part = None
                for j in range(1, c + 1):
                    term = gather(c, j, j + last, ch)
                    part = term if part is None else part + term
                sums[c - 1, :, cols(ch)] = part.astype(jnp.bfloat16)
                sum_copy(c, ch).start()

    for ch in range(nch):
        for k in range(len(PEER_OFFSETS)):
            for slot in range(slabs):
                z_copy(own(slot, ch), slot, ch, k).wait_send()

        @pl.when(s < ns - 1)
        def _():
            for c in range(slabs):
                x_copy(c, ch).wait_send()
            for c in range(1, slabs):
                sum_copy(c, ch).wait_send()
                for k in range(len(PEER_OFFSETS)):
                    z_copy(own(c + last, ch), c + last, ch, k).wait_send()


def per_device(ns, nd, stacked, edges, picks, self_w, neigh_w):
    _, node_rows, width = stacked.shape
    tiles = len(PEER_OFFSETS) + 1
    block = edges.shape[1] // tiles
    slabs = node_rows // block
    nch = max(1, width // 256)
    slots = 2 * slabs - 1
    others = max(1, slabs - 1)
    vmem = pl.BlockSpec(memory_space=pltpu.VMEM)
    hbm = pl.BlockSpec(memory_space=pl.ANY)
    result = pl.pallas_call(
        functools.partial(kernel, ns, nd, slabs, nch),
        out_shape=jax.ShapeDtypeStruct((node_rows, width), jnp.bfloat16),
        in_specs=[vmem, vmem, pl.BlockSpec(memory_space=pltpu.SMEM), hbm, hbm],
        out_specs=vmem,
        scratch_shapes=[
            pltpu.VMEM((width, width), jnp.bfloat16),
            pltpu.VMEM((width, width), jnp.bfloat16),
            pltpu.VMEM((slots, tiles * block, width), jnp.bfloat16),
            pltpu.VMEM((slabs, slabs, block, tiles * block), jnp.bfloat16),
            pltpu.VMEM((block, width), jnp.float32),
            pltpu.VMEM((block, width), jnp.float32),
            pltpu.VMEM((slabs, block, width), jnp.bfloat16),
            pltpu.VMEM((others, block, width), jnp.bfloat16),
            pltpu.VMEM((others, block, width), jnp.bfloat16),
            pltpu.VMEM((others, block, width), jnp.bfloat16),
            pltpu.SemaphoreType.DMA((2,)),
            pltpu.SemaphoreType.DMA((slots, nch, tiles - 1)),
            pltpu.SemaphoreType.DMA((slots, nch, tiles - 1)),
            pltpu.SemaphoreType.DMA((slabs, nch)),
            pltpu.SemaphoreType.DMA((slabs, nch)),
            pltpu.SemaphoreType.DMA((others, nch)),
            pltpu.SemaphoreType.DMA((others, nch)),
        ],
        compiler_params=pltpu.CompilerParams(collective_id=0, has_side_effects=True),
    )(stacked[0], edges, picks, self_w[0], neigh_w[0])
    return result[None]


def solution(mesh):
    in_specs = (
        P("section", "dom", None),
        P("dom", None),
        P("dom", None),
        P("section", None, None),
        P("section", None, None),
    )
    out_specs = P("section", "dom", None)
    ns, nd = mesh.shape["section"], mesh.shape["dom"]
    return jax.shard_map(
        functools.partial(per_device, ns, nd),
        mesh=mesh, in_specs=in_specs, out_specs=out_specs, check_vma=False,
    )
```

profile of v0, /device:TPU:6, one launch (start us, length us, event | category | flops | bytes accessed | tf_op | source)
XLA Modules:
  0.0 51.5 jit_solution(5332416431768162893)
XLA Ops:
  0.0 49.8 %shard_map.55 = bf16[128,1024]{1,0:T(8,128)(2,1)} custom-call(bf16[128,1024]{1,0:T(8,128)(2,1)} %bitcast.7, s32[128,256]{1,0:T(8,128)} %edges.1, s32[2,3]{1,0:T(2,128)} %picks.1, bf16[1024,1024]{1,0:T(8,128)(2,1)} %bitcast.4, bf16[1024,1024]{1,0:T(8,128)(2,1)} %bitcast.5), custom_call_target="tpu_custom_call" | custom-call | tf_op jit(solution)/shard_map/pallas_call | solution.py:285
  49.8 1.7 %copy.7 = bf16[1,128,1024]{2,1,0:T(8,128)(2,1)} copy(bf16[1,128,1024]{2,1,0:T(8,128)(2,1)} %bitcast.6) | data formatting | bytes 524288
where the time goes:
time: 52 us; the launch traced here: 51.5 us
  Pallas kernels  49.8 us (96%)
  local copies, waits for them, and re-layouts  1.67 us (3%)
    pallas_call x1, Pallas kernels, per_device(): pl.pallas_call(functools.partial(kernel, ns, nd, slabs, nch), out_shape=j...  49.8 us
    unnamed x1, local copies, waits for them, and re-layouts  1.67 us

commit v1 on v0

v1 whole, which is shorter than its diff:
```python
import functools

import jax
import jax.numpy as jnp
from jax import lax
from jax.experimental import pallas as pl
from jax.experimental.pallas import tpu as pltpu
from jax.sharding import PartitionSpec as P

PEER_OFFSETS = (-1, 1, 2)
MESH = pl.DeviceIdType.MESH
BELOW, NEXT, FAR = range(3)
QUARTERS, PIECES = 4, 4
VIA = (1, 2)


def plan(nch, slabs):
    return {(j, nch - 1): VIA[j % len(VIA)] for j in range(slabs)}


def kernel(
    ns, nd, slabs, nch,
    stacked, edges_hbm, picks, ws_hbm, wn_hbm, out,
    ws, wn, vs, vn, edges, src, alt, masks, pre, acc, stage, above, sums, below, histsum,
    wsem, insem, outsem, zsend, zrecv, asend, psend, xsend, xrecv, tsend, trecv,
    ssend, srecv, hsend, hrecv, osend, orecv, vsend, vrecv, vpass, bsend, brecv, dsend,
):
    tiles = len(PEER_OFFSETS) + 1
    block = edges.shape[1] // tiles
    width = stacked.shape[1]
    cw = width // nch
    near, distant = list(range(nch // 2)), list(range(nch // 2, nch))
    half = cw * len(near)
    everywhere = list(range(nch))
    detour = plan(nch, slabs)
    last = slabs - 1
    s = lax.axis_index("section")
    p = lax.axis_index("dom")
    odd = lax.rem(p, 2)
    partner = p + 1 - 2 * odd
    across = lax.rem(p - 1 + 2 * odd + nd, nd)
    ahead, behind = lax.rem(p + 2, nd), lax.rem(p + nd - 2, nd)
    quarter = lax.rem(p, QUARTERS)
    twin = jnp.where(quarter < 2, p + 2, p - 2)
    top, helper, under = ns - 1, ns - 2, ns - 3
    is_first, is_top, is_helper = s == 0, s == top, s == helper
    is_mid = (s > 0) & (s <= under)
    sends_up = s <= under

    def at(section, dom):
        return {"section": section, "dom": dom}

    def rows(c):
        return pl.ds(c * block, block)

    def cols(ch):
        return pl.ds(ch * cw, cw)

    def own(slot, ch):
        return src.at[slot, rows(0), cols(ch)]

    def made_slot(c):
        return slabs + c

    def top_hist(j):
        return 2 * slabs - 1 + j

    e_copy = pltpu.make_async_copy(edges_hbm, edges, wsem.at[2])
    w_self = pltpu.make_async_copy(ws_hbm, ws, wsem.at[0])
    w_neigh = pltpu.make_async_copy(wn_hbm, wn, wsem.at[1])

    def given(j, slot):
        return pltpu.make_async_copy(stacked.at[rows(j)], src.at[slot, rows(0)], insem.at[j])

    @pl.when(is_first)
    def _():
        for j in range(slabs):
            given(j, j).start()

    @pl.when(is_mid | is_helper)
    def _():
        for j in range(1, slabs):
            given(j, j).start()

    @pl.when(is_top)
    def _():
        for j in range(1, slabs):
            given(j, top_hist(j)).start()

    barrier = pltpu.get_barrier_semaphore()

    def greet(section, dom):
        pl.semaphore_signal(barrier, inc=1, device_id=at(section, dom), device_id_type=MESH)

    for dom in (ahead, behind, across, partner):
        greet(s, dom)

    @pl.when(is_first)
    def _():
        for v in VIA:
            for dom in (ahead, across):
                greet(v, dom)

    for v in VIA:
        @pl.when(s == v)
        def _():
            greet(0, p)

    @pl.when(is_mid & (s > 1))
    def _():
        greet(s - 1, p)

    @pl.when(is_helper)
    def _():
        greet(top, p)
        greet(under, p)

    @pl.when(is_top)
    def _():
        greet(under, p)
        for dom in (p, ahead, across):
            greet(helper, dom)

    e_copy.start()

    w_self.start()
    w_neigh.start()

    def remote(src_ref, dst_ref, send, recv, section, dom):
        return pltpu.make_async_remote_copy(
            src_ref=src_ref, dst_ref=dst_ref, send_sem=send, recv_sem=recv,
            device_id=at(section, dom), device_id_type=MESH,
        )

    def peer(src_ref, slot, ch, k, sems, section):
        dom = behind if k == FAR else across
        return remote(
            src_ref, src.at[slot, rows(k + 1), cols(ch)],
            sems.at[slot, ch, k], zrecv.at[slot, ch, k], section, dom,
        )

    def spread(src_ref, slot, ch, sems, section, act):
        act(peer(src_ref, slot, ch, FAR, sems, section))

        @pl.when(odd == 1)
        def _():
            act(peer(src_ref, slot, ch, BELOW, sems, section))

    def start(copy):
        copy.start()

    def sent(copy):
        copy.wait_send()

    def share(slot, ch):
        return remote(
            own(slot, ch), src.at[slot, pl.ds((odd + 1) * block, block), cols(ch)],
            psend.at[slot, ch, 0], zrecv.at[slot, ch, odd], s, partner,
        )

    def handed(slot, ch):
        return remote(
            src.at[slot, rows(FAR + 1), cols(ch)], src.at[slot, rows(NEXT + 1), cols(ch)],
            psend.at[slot, ch, 1], zrecv.at[slot, ch, NEXT], s, partner,
        )

    def exchange(slot, ch):
        spread(own(slot, ch), slot, ch, zsend, s, start)
        share(slot, ch).start()

    def left(slot, ch, crossing=True):
        if crossing:
            spread(own(slot, ch), slot, ch, zsend, s, sent)
        sent(share(slot, ch))

    def relayed(slot):
        @pl.when(odd == 0)
        def _():
            for ch in range(nch):
                sent(handed(slot, ch))

    def exchanged(slot, crossing=everywhere):
        for ch in range(nch):
            left(slot, ch, ch in crossing)
        relayed(slot)

    def arrived(slot, ch, k):
        ref = src.at[slot, rows(k + 1), cols(ch)]
        pltpu.make_async_copy(ref, ref, zrecv.at[slot, ch, k]).wait()

    def relay(slot, ch):
        arrived(slot, ch, FAR)

        @pl.when(odd == 0)
        def _():
            handed(slot, ch).start()

    def rest(slot, ch):
        arrived(slot, ch, BELOW)
        arrived(slot, ch, NEXT)

    def up(c, ch, way=0):
        return remote(
            stage.at[c, :, cols(ch)], own(0, ch) if c == 0 else above.at[c - 1, :, cols(ch)],
            xsend.at[way, c, ch], xrecv.at[c, ch], s + 1 + way, p,
        )

    def sum_up(c, ch, way=0):
        return remote(
            sums.at[c - 1, :, cols(ch)], below.at[c - 1, :, cols(ch)],
            ssend.at[way, c - 1, ch], srecv.at[c - 1, ch], s + 1 + way, p,
        )

    def upward(copy, c, ch, act):
        @pl.when(s == under)
        def _():
            act(copy(c, ch, 1))

        act(copy(c, ch))

    def made_up(c, ch):
        return remote(
            stage.at[c, :, cols(ch)], own(made_slot(c), ch), bsend.at[c, ch], brecv.at[c, ch], top, p,
        )

    def lend(j, ch):
        return remote(
            own(j, ch), alt.at[j, :, cols(ch)], tsend.at[j, ch], trecv.at[j, ch], detour[j, ch], p,
        )

    def hist_up(c):
        return remote(sums.at[c], histsum.at[c], hsend.at[c], hrecv.at[c], top, p)

    def hand_back(c):
        return remote(
            src.at[made_slot(c), rows(0), pl.ds(0, half)], out.at[rows(c), pl.ds(0, half)],
            osend.at[c], orecv.at[c], helper, p,
        )

    depth = width // QUARTERS
    bit = depth // PIECES
    pieces = [(m, h) for m in range(2) for h in range(PIECES)]

    def part(pair, m, owner, h):
        return pair[m].at[pl.ds(owner * depth + h * bit, bit), pl.ds(0, half)]

    def weight_up(m, h):
        return remote(
            part((ws_hbm, wn_hbm), m, quarter, h), part((vs, vn), m, quarter, h),
            vsend.at[m, h], vrecv.at[m, 0, h], top, p,
        )

    def weight_pass(m, h, how):
        dom = twin if how == 2 else partner
        ref = part((vs, vn), m, quarter if how < 3 else lax.rem(quarter + 2, QUARTERS), h)
        return remote(ref, ref, vpass.at[m, how - 1, h], vrecv.at[m, how, h], s, dom)

    def weight_wait(m, how, h):
        ref = part((vs, vn), m, 0, h)
        pltpu.make_async_copy(ref, ref, vrecv.at[m, how, h]).wait()

    @pl.when(is_first)
    def _():
        for j in range(slabs):
            given(j, j).wait()

    @pl.when(is_mid | is_helper)
    def _():
        for j in range(1, slabs):
            given(j, j).wait()

    @pl.when(is_top)
    def _():
        for j in range(1, slabs):
            given(j, top_hist(j)).wait()

    def one(flag, amount=1):
        return jnp.where(flag, amount, 0)

    greetings = 4 + one(is_first, len(VIA)) + one(is_mid) + one(s == under) + one(is_helper, 3) + one(is_top)
    for v in VIA:
        greetings = greetings + one(s == v, 2)
    pl.semaphore_wait(barrier, greetings)

    @pl.when(is_first)
    def _():
        for (j, ch) in detour:
            lend(j, ch).start()
        for ch in range(nch):
            for j in range(slabs):
                if (j, ch) not in detour:
                    spread(own(j, ch), j, ch, zsend, s, start)
                share(j, ch).start()

    @pl.when(is_helper)
    def _():
        for m, h in pieces:
            weight_up(m, h).start()

    for v in VIA:
        @pl.when(s == v)
        def _():
            mine = [unit for unit in detour if detour[unit] == v]
            for (j, ch) in mine:
                lend(j, ch).wait_recv()
                spread(alt.at[j, :, cols(ch)], j, ch, asend, 0, start)
            for (j, ch) in mine:
                spread(alt.at[j, :, cols(ch)], j, ch, asend, 0, sent)

    @pl.when(is_mid | is_helper)
    def _():
        for j in range(1, slabs):
            for ch in range(nch):
                exchange(j, ch)

    @pl.when(is_top)
    def _():
        for j in range(1, slabs):
            for ch in range(nch):
                exchange(top_hist(j), ch)

    e_copy.wait()
    tile = lax.broadcasted_iota(jnp.int32, (block, edges.shape[1]), 1) // block
    degree = []
    for c in range(slabs):
        entries = edges[rows(c), :].astype(jnp.float32)
        total = jnp.ones((block, 1), jnp.float32)
        for j in range(slabs):
            scale = jnp.full(entries.shape, 1.0 if c == j else 0.0, jnp.float32)
            for k in range(len(PEER_OFFSETS)):
                wanted = jnp.where(picks[c, k] == j, 1.0, 0.0)
                scale = jnp.where(tile == k + 1, wanted, scale)
            masked = entries * scale
            masks[c, j] = masked.astype(jnp.bfloat16)
            total = total + jnp.sum(masked, axis=1, keepdims=True)
        degree.append(total)

    def gather(c, j, slot, ch):
        return jnp.dot(masks[c, j], src[slot, :, cols(ch)], preferred_element_type=jnp.float32)

    def gathers(c, pairs, ch):
        total = None
        for j, slot in pairs:
            term = gather(c, j, slot, ch)
            total = term if total is None else total + term
        return jnp.zeros((block, cw), jnp.float32) if total is None else total

    def span(chunks):
        return pl.ds(chunks[0] * cw, len(chunks) * cw)

    def self_part(c, ref, weights, chunks=everywhere):
        acc[c, :, span(chunks)] = jnp.dot(
            ref[...], weights[:, span(chunks)], preferred_element_type=jnp.float32
        )

    def finish(c, ch, summed, weights, emit, at_end, chunks=everywhere):
        mean = (summed / degree[c]).astype(jnp.bfloat16)
        if not at_end:
            acc[c, :, span(chunks)] += jnp.dot(
                mean, weights[cols(ch), span(chunks)], preferred_element_type=jnp.float32
            )
            return
        for n in chunks:
            hidden = acc[c, :, cols(n)] + jnp.dot(
                mean, weights[cols(ch), cols(n)], preferred_element_type=jnp.float32
            )
            emit(c, n, jnp.maximum(hidden, 0.0).astype(jnp.bfloat16))

    def put(c, n):
        return pltpu.make_async_copy(
            stage.at[c, :, cols(n)], out.at[rows(c), cols(n)], outsem.at[c, n]
        )

    def emit_up(c, n, made):
        stage[c, :, cols(n)] = made
        if c > 0:
            src[c + last, rows(0), cols(n)] = made
            exchange(c + last, n)
        upward(up, c, n, start)
        put(c, n).start()

    def emit_inner(c, n, made):
        src[made_slot(c), rows(0), cols(n)] = made
        exchange(made_slot(c), n)
        if n == near[-1]:
            hand_back(c).start()

    def emit_across(c, n, made):
        stage[c, :, cols(n)] = made
        made_up(c, n).start()
        spread(stage.at[c, :, cols(n)], made_slot(c), n, dsend, top, start)
        put(c, n).start()

    def emit_out(c, n, made):
        stage[c, :, cols(n)] = made
        put(c, n).start()

    def send_sums(c):
        relay(c + last, 0)
        for ch in range(nch):
            if ch + 1 < nch:
                relay(c + last, ch + 1)
            rest(c + last, ch)
            total = gathers(c, [(j, j + last) for j in range(1, c + 1)], ch)
            sums[c - 1, :, cols(ch)] = total.astype(jnp.bfloat16)
            upward(sum_up, c, ch, start)

    @pl.when(is_first)
    def _():
        w_self.wait()
        for c in range(slabs):
            self_part(c, src.at[c, rows(0)], ws)
        w_neigh.wait()
        everything = [(j, j) for j in range(slabs)]
        for j in range(slabs):
            relay(j, 0)
        for ch in range(nch):
            if ch + 1 < nch:
                for j in range(slabs):
                    relay(j, ch + 1)
            for j in range(slabs):
                rest(j, ch)
            finish(0, ch, gathers(0, everything, ch), wn, emit_up, ch == nch - 1)
        for c in range(1, slabs):
            for ch in range(nch):
                finish(c, ch, gathers(c, everything, ch), wn, emit_up, ch == nch - 1)
            send_sums(c)

    def first_slab_up():
        for ch in range(nch):
            up(0, ch).wait_recv()
            exchange(0, ch)

    def layer_above(w_s, w_n, emit, after, chunks=everywhere):
        self_part(0, src.at[0, rows(0)], w_s, chunks)
        relay(0, 0)
        for ch in range(nch):
            if ch + 1 < nch:
                relay(0, ch + 1)
            rest(0, ch)
            finish(0, ch, pre[0, :, cols(ch)] + gather(0, 0, 0, ch), w_n, emit, ch == nch - 1, chunks)
        for c in range(1, slabs):
            for ch in range(nch):
                pre[c, :, cols(ch)] += gather(c, 0, 0, ch)
            for ch in range(nch):
                up(c, ch).wait_recv()
            self_part(c, above.at[c - 1], w_s, chunks)
            for ch in range(nch):
                sum_up(c, ch).wait_recv()
                finish(
                    c, ch, pre[c, :, cols(ch)] + below[c - 1, :, cols(ch)].astype(jnp.float32),
                    w_n, emit, ch == nch - 1, chunks,
                )
            after(c)

    def take_hist(slot):
        for j in range(1, slabs):
            for ch in range(nch):
                relay(slot(j), ch)
        for j in range(1, slabs):
            for ch in range(nch):
                rest(slot(j), ch)

    def hist_into(slot, keep):
        for c in range(slabs):
            for ch in range(nch):
                keep(c, ch, gathers(c, [(j, slot(j)) for j in range(c + 1, slabs)], ch))

    def keep_pre(c, ch, total):
        pre[c, :, cols(ch)] = total

    def keep_sum(c, ch, total):
        sums[c, :, cols(ch)] = total.astype(jnp.bfloat16)

    @pl.when(is_mid)
    def _():
        take_hist(lambda j: j)
        hist_into(lambda j: j, keep_pre)
        w_self.wait()
        w_neigh.wait()
        first_slab_up()
        layer_above(ws, wn, emit_up, send_sums)

    @pl.when(is_helper)
    def _():
        take_hist(lambda j: j)
        hist_into(lambda j: j, keep_sum)
        for c in range(last):
            hist_up(c).start()
        hist_into(lambda j: j, keep_pre)
        w_self.wait()
        w_neigh.wait()
        first_slab_up()
        layer_above(ws, wn, emit_across, lambda c: None, distant)

    @pl.when(is_top)
    def _():
        take_hist(top_hist)
        for i, (m, h) in enumerate(pieces):
            weight_wait(m, 0, h)
            weight_pass(m, h, 1).start()
            weight_pass(m, h, 2).start()
            if i >= 2:
                weight_wait(pieces[i - 2][0], 2, pieces[i - 2][1])
                weight_pass(*pieces[i - 2], 3).start()
        for m, h in pieces[-2:]:
            weight_wait(m, 2, h)
            weight_pass(m, h, 3).start()
        for j in range(1, slabs):
            exchanged(top_hist(j))
        for m, h in pieces:
            weight_wait(m, 1, h)
            weight_wait(m, 3, h)
        for m, h in pieces:
            for how in (1, 2, 3):
                sent(weight_pass(m, h, how))
        w_self.wait()
        w_neigh.wait()
        first_slab_up()
        for c in range(slabs):
            if c < last:
                hist_up(c).wait_recv()
                pre[c] = histsum[c].astype(jnp.float32)
            else:
                pre[c] = jnp.zeros((block, width), jnp.float32)
        layer_above(vs, vn, emit_inner, lambda c: None, near)
        exchanged(0)
        hist_into(top_hist, keep_pre)
        for c in range(slabs):
            for ch in distant:
                made_up(c, ch).wait_recv()
                share(made_slot(c), ch).start()
            self_part(c, src.at[made_slot(c), rows(0)], ws)
            for j in range(c):
                for ch in range(nch):
                    pre[c, :, cols(ch)] += gather(c, j, made_slot(j), ch)
            for ch in range(nch):
                left(made_slot(c), ch, ch in near)
            sent(hand_back(c))
            order = distant + near
            relay(made_slot(c), order[0])
            for i, ch in enumerate(order):
                if i + 1 < nch:
                    relay(made_slot(c), order[i + 1])
                rest(made_slot(c), ch)
                finish(c, ch, pre[c, :, cols(ch)] + gather(c, c, made_slot(c), ch), wn, emit_out, i == nch - 1)
            relayed(made_slot(c))

    @pl.when(jnp.logical_not(is_helper))
    def _():
        for c in range(slabs):
            for n in range(nch):
                put(c, n).wait()

    @pl.when(is_helper)
    def _():
        for c in range(slabs):
            for ch in distant:
                put(c, ch).wait()
                sent(made_up(c, ch))
                spread(stage.at[c, :, cols(ch)], made_slot(c), ch, dsend, top, sent)

    @pl.when(is_first)
    def _():
        for j in range(slabs):
            for ch in range(nch):
                if (j, ch) in detour:
                    sent(lend(j, ch))
            exchanged(j, [ch for ch in range(nch) if (j, ch) not in detour])

    @pl.when(is_mid | is_helper)
    def _():
        for j in range(1, slabs):
            exchanged(j)
        exchanged(0)

    @pl.when(sends_up)
    def _():
        for ch in range(nch):
            for c in range(slabs):
                upward(up, c, ch, sent)
            for c in range(1, slabs):
                upward(sum_up, c, ch, sent)
        for c in range(1, slabs):
            exchanged(c + last)

    @pl.when(is_helper)
    def _():
        for m, h in pieces:
            sent(weight_up(m, h))
        for c in range(last):
            sent(hist_up(c))
        for c in range(slabs):
            hand_back(c).wait_recv()


def per_device(ns, nd, stacked, edges, picks, self_w, neigh_w):
    _, node_rows, width = stacked.shape
    tiles = len(PEER_OFFSETS) + 1
    block = edges.shape[1] // tiles
    slabs = node_rows // block
    nch = max(1, width // 256)
    slots = 3 * slabs - 1
    others = max(1, slabs - 1)
    anywhere = pl.BlockSpec(memory_space=pl.ANY)
    bf16, f32 = jnp.bfloat16, jnp.float32
    sem = pltpu.SemaphoreType.DMA
    result = pl.pallas_call(
        functools.partial(kernel, ns, nd, slabs, nch),
        out_shape=jax.ShapeDtypeStruct((node_rows, width), bf16),
        in_specs=[anywhere, anywhere, pl.BlockSpec(memory_space=pltpu.SMEM), anywhere, anywhere],
        out_specs=anywhere,
        scratch_shapes=[
            pltpu.VMEM((width, width), bf16),
            pltpu.VMEM((width, width), bf16),
            pltpu.VMEM((width, width // nch * (nch // 2)), bf16),
            pltpu.VMEM((width, width // nch * (nch // 2)), bf16),
            pltpu.VMEM(edges.shape, jnp.int32),
            pltpu.VMEM((slots, tiles * block, width), bf16),
            pltpu.VMEM((slabs, block, width), bf16),
            pltpu.VMEM((slabs, slabs, block, tiles * block), bf16),
            pltpu.VMEM((slabs, block, width), f32),
            pltpu.VMEM((slabs, block, width), f32),
            pltpu.VMEM((slabs, block, width), bf16),
            pltpu.VMEM((others, block, width), bf16),
            pltpu.VMEM((slabs, block, width), bf16),
            pltpu.VMEM((others, block, width), bf16),
            pltpu.VMEM((others, block, width), bf16),
            sem((3,)),
            sem((slabs,)),
            sem((slabs, nch)),
            sem((slots, nch, tiles - 1)),
            sem((slots, nch, tiles - 1)),
            sem((slabs, nch, tiles - 1)),
            sem((slots, nch, 2)),
            sem((2, slabs, nch)),
            sem((slabs, nch)),
            sem((slabs, nch)),
            sem((slabs, nch)),
            sem((2, others, nch)),
            sem((others, nch)),
            sem((others,)),
            sem((others,)),
            sem((slabs,)),
            sem((slabs,)),
            sem((2, PIECES)),
            sem((2, QUARTERS, PIECES)),
            sem((2, QUARTERS - 1, PIECES)),
            sem((slabs, nch)),
            sem((slabs, nch)),
            sem((slots, nch, tiles - 1)),
        ],
        compiler_params=pltpu.CompilerParams(collective_id=0, has_side_effects=True),
    )(stacked[0], edges, picks, self_w[0], neigh_w[0])
    return result[None]


def solution(mesh):
    in_specs = (
        P("section", "dom", None),
        P("dom", None),
        P("dom", None),
        P("section", None, None),
        P("section", None, None),
    )
    out_specs = P("section", "dom", None)
    ns, nd = mesh.shape["section"], mesh.shape["dom"]
    return jax.shard_map(
        functools.partial(per_device, ns, nd),
        mesh=mesh, in_specs=in_specs, out_specs=out_specs, check_vma=False,
    )
```

time: 52 us -> 51.3 us (0.987)
  the two profiles are of different devices: /device:TPU:6 before, /device:TPU:7 now
where the time goes in v1:
time: 51.3 us; the launch traced here: 51.2 us
  Pallas kernels  49.5 us (96%)
  local copies, waits for them, and re-layouts  1.67 us (3%)
    pallas_call x1, Pallas kernels, per_device(): pl.pallas_call(functools.partial(kernel, ns, nd, slabs, nch), out_shape=j...  49.5 us
    unnamed x1, local copies, waits for them, and re-layouts  1.67 us

profile of v1, /device:TPU:7, one launch (start us, length us, event | category | flops | bytes accessed | tf_op | source)
XLA Modules:
  0.0 51.2 jit_solution(10083561396944895006)
XLA Ops:
  0.0 49.5 %shard_map.55 = bf16[128,1024]{1,0:T(8,128)(2,1)} custom-call(bf16[128,1024]{1,0:T(8,128)(2,1)} %bitcast.7, s32[128,256]{1,0:T(8,128)} %edges_hbm.1, s32[2,3]{1,0:T(2,128)} %picks.1, bf16[1024,1024]{1,0:T(8,128)(2,1)} %bitcast.4, bf16[1024,1024]{1,0:T(8,128)(2,1)} %bitcast.5), custom_call_target="tpu_custom_call" | custom-call | tf_op jit(solution)/shard_map/pallas_call | solution.py:608
  49.5 1.7 %copy.7 = bf16[1,128,1024]{2,1,0:T(8,128)(2,1)} copy(bf16[1,128,1024]{2,1,0:T(8,128)(2,1)} %bitcast.6) | data formatting | bytes 524288

commit v2 on v1

v2 whole, which is shorter than its diff:
```python
import functools

import jax
import jax.numpy as jnp
from jax import lax
from jax.experimental import pallas as pl
from jax.experimental.pallas import tpu as pltpu
from jax.sharding import PartitionSpec as P

PEER_OFFSETS = (-1, 1, 2)
MESH = pl.DeviceIdType.MESH
BELOW, NEXT, FAR = range(3)
LANES = 128
QUARTERS, PIECES = 4, 4
VIA = (1, 2)


def plan(width):
    units = width // LANES
    near = units * 5 // 8
    far = units - near
    sizes = [near * 2 // 5, near - near * 2 // 5, far - far // 3, far // 3]
    starts = [sum(sizes[:i]) for i in range(len(sizes))]
    return {
        "sizes": sizes,
        "starts": starts,
        "near": [0, 1],
        "distant": [2, 3],
        "detour": {(0, 2): VIA[0], (1, 2): VIA[1]},
        "given": [0, 1, 3, 2],
        "inner": [0, 2, 1, 3],
        "twice": {3},
        "early": 1,
        "twice_given": {2},
    }


def kernel(
    ns, nd, slabs,
    stacked, edges_hbm, picks, ws_hbm, wn_hbm, out,
    ws, wn, vs, vn, edges, src, alt, masks, pre, acc, stage, above, sums, below, histsum,
    wsem, insem, outsem, gone, zrecv, hrecv, xrecv, arecv, srecv, brecv, trecv, qrecv, orecv,
    vrecv, precv,
):
    tiles = len(PEER_OFFSETS) + 1
    block = edges.shape[1] // tiles
    width = stacked.shape[1]
    how = plan(width)
    sizes, starts, near, distant = (how[key] for key in ("sizes", "starts", "near", "distant"))
    detour = {unit: via for unit, via in how["detour"].items() if unit[0] < slabs}
    everywhere = list(range(len(sizes)))
    half = sum(sizes[ch] for ch in near) * LANES
    last = slabs - 1
    s = lax.axis_index("section")
    p = lax.axis_index("dom")
    odd = lax.rem(p, 2)
    is_odd, is_even = odd == 1, odd == 0
    partner = p + 1 - 2 * odd
    across = lax.rem(p - 1 + 2 * odd + nd, nd)
    ahead, behind = lax.rem(p + 2, nd), lax.rem(p + nd - 2, nd)
    quarter = lax.rem(p, QUARTERS)
    twin = jnp.where(quarter < 2, p + 2, p - 2)
    top, helper, under = ns - 1, ns - 2, ns - 3
    is_first, is_top, is_helper = s == 0, s == top, s == helper
    is_mid = (s > 0) & (s <= under)
    sends_up = s <= under

    def at(section, dom):
        return {"section": section, "dom": dom}

    def rows(c):
        return pl.ds(c * block, block)

    def cols(ch):
        return pl.ds(starts[ch] * LANES, sizes[ch] * LANES)

    def span(chunks):
        return pl.ds(starts[chunks[0]] * LANES, sum(sizes[ch] for ch in chunks) * LANES)

    def own(slot, ch):
        return src.at[slot, rows(0), cols(ch)]

    def made_slot(c):
        return slabs + c

    def hist_slot(j):
        return 2 * slabs - 1 + j

    e_copy = pltpu.make_async_copy(edges_hbm, edges, wsem.at[2])
    w_self = pltpu.make_async_copy(ws_hbm, ws, wsem.at[0])
    w_neigh = pltpu.make_async_copy(wn_hbm, wn, wsem.at[1])

    def given(j, slot):
        return pltpu.make_async_copy(stacked.at[rows(j)], src.at[slot, rows(0)], insem.at[j])

    @pl.when(is_first)
    def _():
        for j in range(slabs):
            given(j, j).start()

    @pl.when(s > 0)
    def _():
        for j in range(1, slabs):
            given(j, hist_slot(j)).start()

    barrier = pltpu.get_barrier_semaphore()

    def greet(section, dom):
        pl.semaphore_signal(barrier, inc=1, device_id=at(section, dom), device_id_type=MESH)

    for dom in (ahead, behind, across, partner):
        greet(s, dom)

    @pl.when(is_first)
    def _():
        for v in VIA:
            for dom in (ahead, across):
                greet(v, dom)

    for v in VIA:
        @pl.when(s == v)
        def _():
            greet(0, p)

    @pl.when(is_mid & (s > 1))
    def _():
        greet(s - 1, p)

    @pl.when(is_helper)
    def _():
        greet(top, p)
        greet(under, p)

    @pl.when(is_top)
    def _():
        greet(under, p)
        for dom in (p, ahead, across):
            greet(helper, dom)

    e_copy.start()
    w_self.start()
    w_neigh.start()

    def remote(src_ref, dst_ref, recv, section, dom, send=0):
        return pltpu.make_async_remote_copy(
            src_ref=src_ref, dst_ref=dst_ref, send_sem=gone.at[send], recv_sem=recv,
            device_id=at(section, dom), device_id_type=MESH,
        )

    def landed(ref, sem):
        pltpu.make_async_copy(ref, ref, sem).wait()

    def drain(units, send=0):
        if units:
            landed(ws.at[pl.ds(0, units * block * LANES // width)], gone.at[send])

    def start(copy):
        copy.start()

    def peer(src_ref, slot, ch, k, section, send):
        dom = behind if k == FAR else across
        return remote(
            src_ref, src.at[slot, rows(k + 1), cols(ch)],
            zrecv.at[slot, ch, 0 if k == FAR else 1], section, dom, send,
        )

    def spread(src_ref, slot, ch, section, twice, send=0):
        start(peer(src_ref, slot, ch, FAR, section, send))

        @pl.when(is_odd)
        def _():
            start(peer(src_ref, slot, ch, BELOW, section, send))

        if ch in twice:
            @pl.when(is_even)
            def _():
                start(peer(src_ref, slot, ch, NEXT, section, send))

    def share(slot, ch):
        start(remote(
            own(slot, ch), src.at[slot, pl.ds((odd + 1) * block, block), cols(ch)],
            zrecv.at[slot, ch, 1], s, partner,
        ))

    def exchange(slot, ch, twice):
        spread(own(slot, ch), slot, ch, s, twice)
        share(slot, ch)

    def relay(slot, ch, twice):
        ref = src.at[slot, rows(FAR + 1), cols(ch)]
        landed(ref, zrecv.at[slot, ch, 0])
        if ch not in twice:
            @pl.when(is_even)
            def _():
                start(remote(
                    ref, src.at[slot, rows(NEXT + 1), cols(ch)], zrecv.at[slot, ch, 1], s, partner,
                ))

    def rest(slot, ch):
        landed(src.at[slot, pl.ds(block, 2 * block), cols(ch)], zrecv.at[slot, ch, 1])

    def hist_send(j):
        slot = hist_slot(j)
        mine = src.at[slot, rows(0)]
        start(remote(mine, src.at[slot, rows(FAR + 1)], hrecv.at[j - 1, 0], s, behind))

        @pl.when(is_odd)
        def _():
            start(remote(mine, src.at[slot, rows(BELOW + 1)], hrecv.at[j - 1, 1], s, across))

        start(remote(
            mine, src.at[slot, pl.ds((odd + 1) * block, block)], hrecv.at[j - 1, 1], s, partner,
        ))

    def hist_take(j):
        slot = hist_slot(j)
        ref = src.at[slot, rows(FAR + 1)]
        landed(ref, hrecv.at[j - 1, 0])

        @pl.when(is_even)
        def _():
            start(remote(ref, src.at[slot, rows(NEXT + 1)], hrecv.at[j - 1, 1], s, partner))

        landed(src.at[slot, pl.ds(block, 2 * block)], hrecv.at[j - 1, 1])

    def upward(src_ref, dst_ref, recv):
        start(remote(src_ref, dst_ref, recv, s + 1, p))

        @pl.when(s == under)
        def _():
            start(remote(src_ref, dst_ref, recv, s + 2, p, 1))

    def up(c, ch):
        part = stage.at[rows(c), cols(ch)]
        if c == 0:
            upward(part, own(0, ch), xrecv.at[ch])
        else:
            upward(part, above.at[c - 1, :, cols(ch)], arecv.at[c - 1])

    def sum_up(c, ch):
        upward(sums.at[c - 1, :, cols(ch)], below.at[c - 1, :, cols(ch)], srecv.at[c - 1, ch])

    def hand_back(c):
        return remote(
            src.at[made_slot(c), rows(0), pl.ds(0, half)], out.at[rows(c), pl.ds(0, half)],
            orecv.at[c], helper, p,
        )

    depth = width // QUARTERS
    bit = depth // PIECES
    pieces = [(m, h) for m in range(2) for h in range(PIECES)]

    def part(pair, m, owner, h):
        return pair[m].at[pl.ds(owner * depth + h * bit, bit), pl.ds(0, half)]

    def weight_up(m, h):
        start(remote(
            part((ws_hbm, wn_hbm), m, quarter, h), part((vs, vn), m, quarter, h),
            vrecv.at[0, m, h], top, p, 1,
        ))

    def weight_pass(m, h, dom, sem, owner, send=1):
        ref = part((vs, vn), m, owner, h)
        start(remote(ref, ref, sem, s, dom, send))

    @pl.when(is_first)
    def _():
        for j in range(slabs):
            given(j, j).wait()

    @pl.when(s > 0)
    def _():
        for j in range(1, slabs):
            given(j, hist_slot(j)).wait()

    def one(flag, amount=1):
        return jnp.where(flag, amount, 0)

    greetings = 4 + one(is_first, len(VIA)) + one(is_mid) + one(s == under) + one(is_helper, 3) + one(is_top)
    for v in VIA:
        greetings = greetings + one(s == v, 2)
    pl.semaphore_wait(barrier, greetings)

    def twice_given(j):
        return [ch for ch in how["twice_given"] if (j, ch) in detour]

    @pl.when(is_first)
    def _():
        for (j, ch), v in detour.items():
            start(remote(own(j, ch), alt.at[j, :, cols(ch)], trecv.at[j, ch], v, p))
        for ch in everywhere:
            for j in range(slabs):
                if (j, ch) not in detour:
                    spread(own(j, ch), j, ch, s, twice_given(j))
                share(j, ch)

    @pl.when(is_helper)
    def _():
        for m, h in pieces:
            weight_up(m, h)

    for v in VIA:
        @pl.when(s == v)
        def _():
            for (j, ch), via in detour.items():
                if via == v:
                    ref = alt.at[j, :, cols(ch)]
                    landed(ref, trecv.at[j, ch])
                    spread(ref, j, ch, 0, twice_given(j), 2)
            count = [sum(sizes[ch] for (j, ch), via in detour.items() if via == v), 0]
            count[1] = sum(
                sizes[ch] for (j, ch), via in detour.items() if via == v and ch in twice_given(j)
            )

            @pl.when(is_odd)
            def _():
                drain(2 * count[0], 2)

            @pl.when(is_even)
            def _():
                drain(count[0] + count[1], 2)

    @pl.when(s > 0)
    def _():
        for j in range(1, slabs):
            hist_send(j)

    e_copy.wait()
    tile = lax.broadcasted_iota(jnp.int32, (block, edges.shape[1]), 1) // block
    degree = []
    for c in range(slabs):
        entries = edges[rows(c), :].astype(jnp.float32)
        total = jnp.ones((block, 1), jnp.float32)
        for j in range(slabs):
            scale = jnp.full(entries.shape, 1.0 if c == j else 0.0, jnp.float32)
            for k in range(len(PEER_OFFSETS)):
                wanted = jnp.where(picks[c, k] == j, 1.0, 0.0)
                scale = jnp.where(tile == k + 1, wanted, scale)
            masked = entries * scale
            masks[j, rows(c)] = masked.astype(jnp.bfloat16)
            total = total + jnp.sum(masked, axis=1, keepdims=True)
        degree.append(total)

    degrees = jnp.concatenate(degree, axis=0)

    def gather(j, slot, ch, dest=slice(None)):
        return jnp.dot(masks[j, dest], src[slot, :, cols(ch)], preferred_element_type=jnp.float32)

    def gathers(pairs, ch, dest=slice(None)):
        total = None
        for j, slot in pairs:
            term = gather(j, slot, ch, dest)
            total = term if total is None else total + term
        return total

    def own_rows(slots):
        return jnp.concatenate([src[slot, rows(0), :] for slot in slots], axis=0)

    def self_part(c, ref, weights, chunks=everywhere):
        acc[rows(c), span(chunks)] = jnp.dot(
            ref[...], weights[:, span(chunks)], preferred_element_type=jnp.float32
        )

    def finish_all(ch, summed, weights, emit, at_end):
        mean = (summed / degrees).astype(jnp.bfloat16)
        if not at_end:
            acc[...] += jnp.dot(mean, weights[cols(ch), :], preferred_element_type=jnp.float32)
            return
        for c in range(slabs):
            for n in everywhere:
                hidden = acc[rows(c), cols(n)] + jnp.dot(
                    mean[c * block:(c + 1) * block], weights[cols(ch), cols(n)],
                    preferred_element_type=jnp.float32,
                )
                emit(c, n, jnp.maximum(hidden, 0.0).astype(jnp.bfloat16))

    def finish(c, ch, summed, weights, emit, at_end, chunks=everywhere):
        mean = (summed / degree[c]).astype(jnp.bfloat16)
        if not at_end:
            acc[rows(c), span(chunks)] += jnp.dot(
                mean, weights[cols(ch), span(chunks)], preferred_element_type=jnp.float32
            )
            return
        for n in chunks:
            hidden = acc[rows(c), cols(n)] + jnp.dot(
                mean, weights[cols(ch), cols(n)], preferred_element_type=jnp.float32
            )
            emit(c, n, jnp.maximum(hidden, 0.0).astype(jnp.bfloat16))

    def put(c, n):
        start(pltpu.make_async_copy(stage.at[rows(c), cols(n)], out.at[rows(c), cols(n)], outsem.at[0]))

    def emit_up(c, n, made):
        stage[rows(c), cols(n)] = made
        if c > 0:
            src[c + last, rows(0), cols(n)] = made
            exchange(c + last, n, how["twice"])
        up(c, n)
        put(c, n)

    def emit_inner(c, n, made):
        src[made_slot(c), rows(0), cols(n)] = made
        exchange(made_slot(c), n, how["twice"])
        if n == near[-1]:
            start(hand_back(c))

    def emit_across(c, n, made):
        stage[rows(c), cols(n)] = made
        part = stage.at[rows(c), cols(n)]
        start(remote(part, own(made_slot(c), n), brecv.at[c, distant.index(n)], top, p))
        spread(part, made_slot(c), n, top, how["twice"])
        put(c, n)

    def emit_out(c, n, made):
        stage[rows(c), cols(n)] = made
        put(c, n)

    def in_turn(order, ready, use):
        ready(order[0])
        for i, ch in enumerate(order):
            if i + 1 < len(order):
                ready(order[i + 1])
            use(ch, i == len(order) - 1)

    def send_sums(c):
        def ready(ch):
            relay(c + last, ch, how["twice"])

        def use(ch, at_end):
            rest(c + last, ch)
            total = gathers([(j, j + last) for j in range(1, c + 1)], ch, rows(c))
            sums[c - 1, :, cols(ch)] = total.astype(jnp.bfloat16)
            sum_up(c, ch)

        in_turn(everywhere, ready, use)

    @pl.when(is_first)
    def _():
        w_self.wait()
        acc[...] = jnp.dot(own_rows(range(slabs)), ws[...], preferred_element_type=jnp.float32)
        w_neigh.wait()

        def ready(ch):
            for j in range(slabs):
                relay(j, ch, twice_given(j))

        def use(ch, at_end):
            for j in range(slabs):
                rest(j, ch)
            finish_all(ch, gathers([(j, j) for j in range(slabs)], ch), wn, emit_up, at_end)

        in_turn(how["given"], ready, use)
        for c in range(1, slabs):
            send_sums(c)

    def first_slab_up():
        for ch in everywhere:
            landed(own(0, ch), xrecv.at[ch])
            exchange(0, ch, how["twice"])

    def layer_above(w_s, w_n, emit, after, chunks=everywhere):
        first_slab_up()
        self_part(0, src.at[0, rows(0)], w_s, chunks)

        def ready(ch):
            relay(0, ch, how["twice"])

        def use(ch, at_end):
            if ch == everywhere[how["early"]]:
                for c in range(1, slabs):
                    landed(above.at[c - 1], arecv.at[c - 1])
                    self_part(c, above.at[c - 1], w_s, chunks)
            rest(0, ch)
            total = pre[:, cols(ch)] + gather(0, 0, ch)
            pre[:, cols(ch)] = total
            finish(0, ch, total[:block], w_n, emit, at_end, chunks)

        in_turn(everywhere, ready, use)
        for c in range(1, slabs):
            for ch in everywhere:
                landed(below.at[c - 1, :, cols(ch)], srecv.at[c - 1, ch])
                finish(
                    c, ch, pre[rows(c), cols(ch)] + below[c - 1, :, cols(ch)].astype(jnp.float32),
                    w_n, emit, ch == everywhere[-1], chunks,
                )
            after(c)

    def hist_sums():
        for c in range(last):
            pre[rows(c)] = jnp.dot(
                masks[c + 1, rows(c)], src[hist_slot(c + 1)], preferred_element_type=jnp.float32
            )
            for j in range(c + 2, slabs):
                pre[rows(c)] += jnp.dot(
                    masks[j, rows(c)], src[hist_slot(j)], preferred_element_type=jnp.float32
                )
        pre[rows(last)] = jnp.zeros((block, width), jnp.float32)

    @pl.when(is_mid)
    def _():
        for j in range(1, slabs):
            hist_take(j)
        hist_sums()
        w_self.wait()
        w_neigh.wait()
        layer_above(ws, wn, emit_up, send_sums)

    @pl.when(is_helper)
    def _():
        for j in range(1, slabs):
            hist_take(j)
        hist_sums()
        for c in range(last):
            sums[c] = pre[rows(c)].astype(jnp.bfloat16)
            start(remote(sums.at[c], histsum.at[c], qrecv.at[c], top, p))
        w_self.wait()
        w_neigh.wait()
        layer_above(ws, wn, emit_across, lambda c: None, distant)

    @pl.when(is_top)
    def _():
        for m, h in pieces:
            landed(part((vs, vn), m, 0, h), vrecv.at[0, m, h])
            weight_pass(m, h, partner, precv.at[0], quarter)
            weight_pass(m, h, twin, vrecv.at[1, m, h], quarter, 2)
        for j in range(1, slabs):
            hist_take(j)
        for m, h in pieces:
            landed(part((vs, vn), m, 0, h), vrecv.at[1, m, h])
            weight_pass(m, h, partner, precv.at[1], lax.rem(quarter + 2, QUARTERS))
        everything = 2 * depth * half // (block * LANES)
        for i in range(2):
            landed(vs.at[pl.ds(0, 2 * depth), pl.ds(0, half)], precv.at[i])
        drain(2 * everything, 1)
        drain(everything, 2)
        for c in range(slabs):
            if c < last:
                landed(histsum.at[c], qrecv.at[c])
                pre[rows(c)] = histsum[c].astype(jnp.float32)
            else:
                pre[rows(c)] = jnp.zeros((block, width), jnp.float32)
        w_self.wait()
        w_neigh.wait()
        layer_above(vs, vn, emit_inner, lambda c: None, near)
        hist_sums()
        slots = [made_slot(c) for c in range(slabs)]

        def given_up(c):
            for ch in distant:
                landed(own(slots[c], ch), brecv.at[c, distant.index(ch)])
                share(slots[c], ch)

        for c in range(last):
            given_up(c)
            for ch in how["inner"]:
                relay(slots[c], ch, how["twice"])
        given_up(last)
        acc[...] = jnp.dot(own_rows(slots), ws[...], preferred_element_type=jnp.float32)

        def ready(ch):
            relay(slots[last], ch, how["twice"])

        def use(ch, at_end):
            for c in range(slabs):
                rest(slots[c], ch)
            total = pre[:, cols(ch)]
            for c in range(slabs):
                term = gather(c, slots[c], ch, pl.ds(c * block, (slabs - c) * block))
                if c > 0:
                    term = jnp.concatenate([jnp.zeros((c * block, term.shape[1]), jnp.float32), term], axis=0)
                total = total + term
            finish_all(ch, total, wn, emit_out, at_end)

        in_turn(how["inner"], ready, use)

    full = sum(sizes)
    part_units = sum(sizes[ch] for ch in distant)
    relayed_units = sum(sizes[ch] for ch in distant if ch not in how["twice"])

    def by_parity(even, odd_units):
        @pl.when(is_even)
        def _():
            drain(even)

        @pl.when(is_odd)
        def _():
            drain(odd_units)

    @pl.when(jnp.logical_not(is_helper))
    def _():
        landed(stage, outsem.at[0])

    @pl.when(is_first)
    def _():
        detoured = sum(sizes[ch] for _, ch in detour)
        twice_units = sum(sizes[ch] for j, ch in detour if ch in twice_given(j))
        base = 3 * full * slabs + full * slabs + last * 4 * full
        by_parity(base - twice_units, base - detoured)

    @pl.when(is_mid)
    def _():
        drain(3 * full * slabs + full * slabs + last * 4 * full)

    @pl.when(s == under)
    def _():
        @pl.when(sends_up)
        def _():
            drain(full * slabs + last * full, 1)

    @pl.when(is_helper)
    def _():
        landed(stage.at[:, span(distant)], outsem.at[0])
        drain(2 * depth * half // (block * LANES), 1)
        twice_units = part_units - relayed_units
        base = 3 * full * slabs + last * full + 2 * part_units * slabs
        by_parity(base + twice_units * slabs, base + part_units * slabs)
        for c in range(slabs):
            hand_back(c).wait_recv()

    @pl.when(is_top)
    def _():
        near_units = full - part_units
        base = 3 * full * slabs + 4 * near_units * slabs + part_units * slabs
        by_parity(base + relayed_units * slabs, base)


def per_device(ns, nd, stacked, edges, picks, self_w, neigh_w):
    _, node_rows, width = stacked.shape
    tiles = len(PEER_OFFSETS) + 1
    block = edges.shape[1] // tiles
    slabs = node_rows // block
    slots = 3 * slabs - 1
    others = max(1, slabs - 1)
    how = plan(width)
    nch = len(how["sizes"])
    half = sum(how["sizes"][ch] for ch in how["near"]) * LANES
    anywhere = pl.BlockSpec(memory_space=pl.ANY)
    bf16, f32 = jnp.bfloat16, jnp.float32
    sem = pltpu.SemaphoreType.DMA
    result = pl.pallas_call(
        functools.partial(kernel, ns, nd, slabs),
        out_shape=jax.ShapeDtypeStruct((node_rows, width), bf16),
        in_specs=[anywhere, anywhere, pl.BlockSpec(memory_space=pltpu.SMEM), anywhere, anywhere],
        out_specs=anywhere,
        scratch_shapes=[
            pltpu.VMEM((width, width), bf16),
            pltpu.VMEM((width, width), bf16),
            pltpu.VMEM((width, half), bf16),
            pltpu.VMEM((width, half), bf16),
            pltpu.VMEM(edges.shape, jnp.int32),
            pltpu.VMEM((slots, tiles * block, width), bf16),
            pltpu.VMEM((slabs, block, width), bf16),
            pltpu.VMEM((slabs, slabs * block, tiles * block), bf16),
            pltpu.VMEM((slabs * block, width), f32),
            pltpu.VMEM((slabs * block, width), f32),
            pltpu.VMEM((slabs * block, width), bf16),
            pltpu.VMEM((others, block, width), bf16),
            pltpu.VMEM((slabs, block, width), bf16),
            pltpu.VMEM((others, block, width), bf16),
            pltpu.VMEM((others, block, width), bf16),
            sem((3,)),
            sem((slabs,)),
            sem((1,)),
            sem((3,)),
            sem((2 * slabs, nch, 2)),
            sem((others, 2)),
            sem((nch,)),
            sem((others,)),
            sem((others, nch)),
            sem((slabs, len(how["distant"]))),
            sem((slabs, nch)),
            sem((others,)),
            sem((slabs,)),
            sem((2, 2, PIECES)),
            sem((2,)),
        ],
        compiler_params=pltpu.CompilerParams(collective_id=0, has_side_effects=True),
    )(stacked[0], edges, picks, self_w[0], neigh_w[0])
    return result[None]


def solution(mesh):
    in_specs = (
        P("section", "dom", None),
        P("dom", None),
        P("dom", None),
        P("section", None, None),
        P("section", None, None),
    )
    out_specs = P("section", "dom", None)
    ns, nd = mesh.shape["section"], mesh.shape["dom"]
    return jax.shard_map(
        functools.partial(per_device, ns, nd),
        mesh=mesh, in_specs=in_specs, out_specs=out_specs, check_vma=False,
    )
```

time: 51.3 us -> 46.4 us (0.904)
  the two profiles are of different devices: /device:TPU:7 before, /device:TPU:6 now
where the time goes in v2:
time: 46.4 us; the launch traced here: 45.6 us
  Pallas kernels  43.9 us (95%)
  local copies, waits for them, and re-layouts  1.67 us (4%)
    pallas_call x1, Pallas kernels, per_device(): pl.pallas_call(functools.partial(kernel, ns, nd, slabs), out_shape=jax.Sh...  43.9 us
    unnamed x1, local copies, waits for them, and re-layouts  1.67 us

profile of v2, /device:TPU:6, one launch (start us, length us, event | category | flops | bytes accessed | tf_op | source)
XLA Modules:
  0.0 45.6 jit_solution(4952805456951890333)
XLA Ops:
  0.0 43.9 %shard_map.55 = bf16[128,1024]{1,0:T(8,128)(2,1)} custom-call(bf16[128,1024]{1,0:T(8,128)(2,1)} %bitcast.7, s32[128,256]{1,0:T(8,128)} %edges_hbm.1, s32[2,3]{1,0:T(2,128)} %picks.1, bf16[1024,1024]{1,0:T(8,128)(2,1)} %bitcast.4, bf16[1024,1024]{1,0:T(8,128)(2,1)} %bitcast.5), custom_call_target="tpu_custom_call" | custom-call | tf_op jit(solution)/shard_map/pallas_call | solution.py:640
  43.9 1.7 %copy.7 = bf16[1,128,1024]{2,1,0:T(8,128)(2,1)} copy(bf16[1,128,1024]{2,1,0:T(8,128)(2,1)} %bitcast.6) | data formatting | bytes 524288

commit v3 on v2

--- a/solution.py
+++ b/solution.py
@@ -28,7 +28,6 @@
         "distant": [2, 3],
         "detour": {(0, 2): VIA[0], (1, 2): VIA[1]},
         "given": [0, 1, 3, 2],
-        "inner": [0, 2, 1, 3],
         "twice": {3},
         "early": 1,
         "twice_given": {2},
@@ -307,18 +306,6 @@
                     ref = alt.at[j, :, cols(ch)]
                     landed(ref, trecv.at[j, ch])
                     spread(ref, j, ch, 0, twice_given(j), 2)
-            count = [sum(sizes[ch] for (j, ch), via in detour.items() if via == v), 0]
-            count[1] = sum(
-                sizes[ch] for (j, ch), via in detour.items() if via == v and ch in twice_given(j)
-            )
-
-            @pl.when(is_odd)
-            def _():
-                drain(2 * count[0], 2)
-
-            @pl.when(is_even)
-            def _():
-                drain(count[0] + count[1], 2)
 
     @pl.when(s > 0)
     def _():
@@ -458,8 +445,9 @@
             landed(own(0, ch), xrecv.at[ch])
             exchange(0, ch, how["twice"])
 
-    def layer_above(w_s, w_n, emit, after, chunks=everywhere):
+    def layer_above(w_s, w_n, emit, after, chunks=everywhere, weights_in=lambda: None):
         first_slab_up()
+        weights_in()
         self_part(0, src.at[0, rows(0)], w_s, chunks)
 
         def ready(ch):
@@ -529,10 +517,11 @@
             landed(part((vs, vn), m, 0, h), vrecv.at[1, m, h])
             weight_pass(m, h, partner, precv.at[1], lax.rem(quarter + 2, QUARTERS))
         everything = 2 * depth * half // (block * LANES)
-        for i in range(2):
-            landed(vs.at[pl.ds(0, 2 * depth), pl.ds(0, half)], precv.at[i])
-        drain(2 * everything, 1)
-        drain(everything, 2)
+
+        def weights_in():
+            for i in range(2):
+                landed(vs.at[pl.ds(0, 2 * depth), pl.ds(0, half)], precv.at[i])
+
         for c in range(slabs):
             if c < last:
                 landed(histsum.at[c], qrecv.at[c])
@@ -541,7 +530,9 @@
                 pre[rows(c)] = jnp.zeros((block, width), jnp.float32)
         w_self.wait()
         w_neigh.wait()
-        layer_above(vs, vn, emit_inner, lambda c: None, near)
+        layer_above(vs, vn, emit_inner, lambda c: None, near, weights_in)
+        drain(2 * everything, 1)
+        drain(everything, 2)
         hist_sums()
         slots = [made_slot(c) for c in range(slabs)]
 
@@ -550,17 +541,11 @@
                 landed(own(slots[c], ch), brecv.at[c, distant.index(ch)])
                 share(slots[c], ch)
 
-        for c in range(last):
-            given_up(c)
-            for ch in how["inner"]:
+        def relays(c, chunks):
+            for ch in chunks:
                 relay(slots[c], ch, how["twice"])
-        given_up(last)
-        acc[...] = jnp.dot(own_rows(slots), ws[...], preferred_element_type=jnp.float32)
-
-        def ready(ch):
-            relay(slots[last], ch, how["twice"])
-
-        def use(ch, at_end):
+
+        def use(ch, at_end=False):
             for c in range(slabs):
                 rest(slots[c], ch)
             total = pre[:, cols(ch)]
@@ -571,7 +556,19 @@
                 total = total + term
             finish_all(ch, total, wn, emit_out, at_end)
 
-        in_turn(how["inner"], ready, use)
+        def own_part(chunks):
+            mine = jnp.concatenate([src[slot, rows(0), span(chunks)] for slot in slots], axis=0)
+            return jnp.dot(mine, ws[span(chunks), :], preferred_element_type=jnp.float32)
+
+        acc[...] = own_part(near)
+        for c in range(slabs):
+            relays(c, near)
+        for c in range(slabs):
+            given_up(c)
+            relays(c, distant)
+        acc[...] += own_part(distant)
+        for ch in everywhere:
+            use(ch, ch == everywhere[-1])
 
     full = sum(sizes)
     part_units = sum(sizes[ch] for ch in distant)
@@ -589,6 +586,22 @@
     @pl.when(jnp.logical_not(is_helper))
     def _():
         landed(stage, outsem.at[0])
+
+    for v in VIA:
+        @pl.when(s == v)
+        def _():
+            count = [sum(sizes[ch] for (j, ch), via in detour.items() if via == v), 0]
+            count[1] = sum(
+                sizes[ch] for (j, ch), via in detour.items() if via == v and ch in twice_given(j)
+            )
+
+            @pl.when(is_odd)
+            def _():
+                drain(2 * count[0], 2)
+
+            @pl.when(is_even)
+            def _():
+                drain(count[0] + count[1], 2)
 
     @pl.when(is_first)
     def _():

time: 46.4 us -> 45.7 us (0.985); the launches traced: 45.6 us -> 45.5 us
  no operation moved by 1% of the time
where the time goes in v3:
time: 45.7 us; the launch traced here: 45.5 us
  Pallas kernels  43.8 us (96%)
  local copies, waits for them, and re-layouts  1.67 us (4%)
    pallas_call x1, Pallas kernels, per_device(): pl.pallas_call(functools.partial(kernel, ns, nd, slabs), out_shape=jax.Sh...  43.8 us
    unnamed x1, local copies, waits for them, and re-layouts  1.67 us

profile of v3, /device:TPU:6, one launch (start us, length us, event | category | flops | bytes accessed | tf_op | source)
XLA Modules:
  0.0 45.5 jit_solution(9062581694099019953)
XLA Ops:
  0.0 43.8 %shard_map.55 = bf16[128,1024]{1,0:T(8,128)(2,1)} custom-call(bf16[128,1024]{1,0:T(8,128)(2,1)} %bitcast.7, s32[128,256]{1,0:T(8,128)} %edges_hbm.1, s32[2,3]{1,0:T(2,128)} %picks.1, bf16[1024,1024]{1,0:T(8,128)(2,1)} %bitcast.4, bf16[1024,1024]{1,0:T(8,128)(2,1)} %bitcast.5), custom_call_target="tpu_custom_call" | custom-call | tf_op jit(solution)/shard_map/pallas_call | solution.py:653
  43.9 1.7 %copy.7 = bf16[1,128,1024]{2,1,0:T(8,128)(2,1)} copy(bf16[1,128,1024]{2,1,0:T(8,128)(2,1)} %bitcast.6) | data formatting | bytes 524288

commit v4 on v3

--- a/solution.py
+++ b/solution.py
@@ -85,6 +85,9 @@
     def hist_slot(j):
         return 2 * slabs - 1 + j
 
+    def lane(slot):
+        return 1 if slot == 2 * slabs - 1 else slot
+
     e_copy = pltpu.make_async_copy(edges_hbm, edges, wsem.at[2])
     w_self = pltpu.make_async_copy(ws_hbm, ws, wsem.at[0])
     w_neigh = pltpu.make_async_copy(wn_hbm, wn, wsem.at[1])
@@ -160,7 +163,7 @@
         dom = behind if k == FAR else across
         return remote(
             src_ref, src.at[slot, rows(k + 1), cols(ch)],
-            zrecv.at[slot, ch, 0 if k == FAR else 1], section, dom, send,
+            zrecv.at[lane(slot), ch, 0 if k == FAR else 1], section, dom, send,
         )
 
     def spread(src_ref, slot, ch, section, twice, send=0):
@@ -178,7 +181,7 @@
     def share(slot, ch):
         start(remote(
             own(slot, ch), src.at[slot, pl.ds((odd + 1) * block, block), cols(ch)],
-            zrecv.at[slot, ch, 1], s, partner,
+            zrecv.at[lane(slot), ch, 1], s, partner,
         ))
 
     def exchange(slot, ch, twice):
@@ -187,16 +190,16 @@
 
     def relay(slot, ch, twice):
         ref = src.at[slot, rows(FAR + 1), cols(ch)]
-        landed(ref, zrecv.at[slot, ch, 0])
+        landed(ref, zrecv.at[lane(slot), ch, 0])
         if ch not in twice:
             @pl.when(is_even)
             def _():
                 start(remote(
-                    ref, src.at[slot, rows(NEXT + 1), cols(ch)], zrecv.at[slot, ch, 1], s, partner,
+                    ref, src.at[slot, rows(NEXT + 1), cols(ch)], zrecv.at[lane(slot), ch, 1], s, partner,
                 ))
 
     def rest(slot, ch):
-        landed(src.at[slot, pl.ds(block, 2 * block), cols(ch)], zrecv.at[slot, ch, 1])
+        landed(src.at[slot, pl.ds(block, 2 * block), cols(ch)], zrecv.at[lane(slot), ch, 1])
 
     def hist_send(j):
         slot = hist_slot(j)
@@ -286,7 +289,7 @@
     @pl.when(is_first)
     def _():
         for (j, ch), v in detour.items():
-            start(remote(own(j, ch), alt.at[j, :, cols(ch)], trecv.at[j, ch], v, p))
+            start(remote(own(j, ch), alt.at[j, :, cols(ch)], trecv.at[j], v, p))
         for ch in everywhere:
             for j in range(slabs):
                 if (j, ch) not in detour:
@@ -304,7 +307,7 @@
             for (j, ch), via in detour.items():
                 if via == v:
                     ref = alt.at[j, :, cols(ch)]
-                    landed(ref, trecv.at[j, ch])
+                    landed(ref, trecv.at[j])
                     spread(ref, j, ch, 0, twice_given(j), 2)
 
     @pl.when(s > 0)
@@ -374,8 +377,10 @@
             )
             emit(c, n, jnp.maximum(hidden, 0.0).astype(jnp.bfloat16))
 
-    def put(c, n):
-        start(pltpu.make_async_copy(stage.at[rows(c), cols(n)], out.at[rows(c), cols(n)], outsem.at[0]))
+    def put(c, chunks):
+        start(pltpu.make_async_copy(
+            stage.at[rows(c), span(chunks)], out.at[rows(c), span(chunks)], outsem.at[0]
+        ))
 
     def emit_up(c, n, made):
         stage[rows(c), cols(n)] = made
@@ -383,7 +388,8 @@
             src[c + last, rows(0), cols(n)] = made
             exchange(c + last, n, how["twice"])
         up(c, n)
-        put(c, n)
+        if n == everywhere[-1]:
+            put(c, everywhere)
 
     def emit_inner(c, n, made):
         src[made_slot(c), rows(0), cols(n)] = made
@@ -396,11 +402,12 @@
         part = stage.at[rows(c), cols(n)]
         start(remote(part, own(made_slot(c), n), brecv.at[c, distant.index(n)], top, p))
         spread(part, made_slot(c), n, top, how["twice"])
-        put(c, n)
+        if n == distant[-1]:
+            put(c, distant)
 
     def emit_out(c, n, made):
         stage[rows(c), cols(n)] = made
-        put(c, n)
+        put(c, [n])
 
     def in_turn(order, ready, use):
         ready(order[0])
@@ -675,13 +682,13 @@
             sem((slabs,)),
             sem((1,)),
             sem((3,)),
-            sem((2 * slabs, nch, 2)),
+            sem((max(2, 2 * slabs - 1), nch, 2)),
             sem((others, 2)),
             sem((nch,)),
             sem((others,)),
             sem((others, nch)),
             sem((slabs, len(how["distant"]))),
-            sem((slabs, nch)),
+            sem((slabs,)),
             sem((others,)),
             sem((slabs,)),
             sem((2, 2, PIECES)),

time: 45.7 us -> 45.6 us (level)
  no operation moved by 1% of the time
where the time goes in v4:
time: 45.6 us; the launch traced here: 45.4 us
  Pallas kernels  43.7 us (96%)
  local copies, waits for them, and re-layouts  1.67 us (4%)
    pallas_call x1, Pallas kernels, per_device(): pl.pallas_call(functools.partial(kernel, ns, nd, slabs), out_shape=jax.Sh...  43.7 us
    unnamed x1, local copies, waits for them, and re-layouts  1.67 us

profile of v4, /device:TPU:6, one launch (start us, length us, event | category | flops | bytes accessed | tf_op | source)
XLA Modules:
  0.0 45.4 jit_solution(1359942316773850120)
XLA Ops:
  0.0 43.7 %shard_map.55 = bf16[128,1024]{1,0:T(8,128)(2,1)} custom-call(bf16[128,1024]{1,0:T(8,128)(2,1)} %bitcast.7, s32[128,256]{1,0:T(8,128)} %edges_hbm.1, s32[2,3]{1,0:T(2,128)} %picks.1, bf16[1024,1024]{1,0:T(8,128)(2,1)} %bitcast.4, bf16[1024,1024]{1,0:T(8,128)(2,1)} %bitcast.5), custom_call_target="tpu_custom_call" | custom-call | tf_op jit(solution)/shard_map/pallas_call | solution.py:660
  43.7 1.7 %copy.7 = bf16[1,128,1024]{2,1,0:T(8,128)(2,1)} copy(bf16[1,128,1024]{2,1,0:T(8,128)(2,1)} %bitcast.6) | data formatting | bytes 524288

commit v5 on v4

--- a/solution.py
+++ b/solution.py
@@ -11,7 +11,7 @@
 MESH = pl.DeviceIdType.MESH
 BELOW, NEXT, FAR = range(3)
 LANES = 128
-QUARTERS, PIECES = 4, 4
+QUARTERS, PIECES = 4, 2
 VIA = (1, 2)
 
 
@@ -393,7 +393,7 @@
 
     def emit_inner(c, n, made):
         src[made_slot(c), rows(0), cols(n)] = made
-        exchange(made_slot(c), n, how["twice"])
+        exchange(made_slot(c), n, ())
         if n == near[-1]:
             start(hand_back(c))
 
@@ -401,7 +401,7 @@
         stage[rows(c), cols(n)] = made
         part = stage.at[rows(c), cols(n)]
         start(remote(part, own(made_slot(c), n), brecv.at[c, distant.index(n)], top, p))
-        spread(part, made_slot(c), n, top, how["twice"])
+        spread(part, made_slot(c), n, top, ())
         if n == distant[-1]:
             put(c, distant)
 
@@ -550,7 +550,7 @@
 
         def relays(c, chunks):
             for ch in chunks:
-                relay(slots[c], ch, how["twice"])
+                relay(slots[c], ch, ())
 
         def use(ch, at_end=False):
             for c in range(slabs):
@@ -579,7 +579,6 @@
 
     full = sum(sizes)
     part_units = sum(sizes[ch] for ch in distant)
-    relayed_units = sum(sizes[ch] for ch in distant if ch not in how["twice"])
 
     def by_parity(even, odd_units):
         @pl.when(is_even)
@@ -631,9 +630,8 @@
     def _():
         landed(stage.at[:, span(distant)], outsem.at[0])
         drain(2 * depth * half // (block * LANES), 1)
-        twice_units = part_units - relayed_units
         base = 3 * full * slabs + last * full + 2 * part_units * slabs
-        by_parity(base + twice_units * slabs, base + part_units * slabs)
+        by_parity(base, base + part_units * slabs)
         for c in range(slabs):
             hand_back(c).wait_recv()
 
@@ -641,7 +639,7 @@
     def _():
         near_units = full - part_units
         base = 3 * full * slabs + 4 * near_units * slabs + part_units * slabs
-        by_parity(base + relayed_units * slabs, base)
+        by_parity(base + part_units * slabs, base)
 
 
 def per_device(ns, nd, stacked, edges, picks, self_w, neigh_w):

time: 45.6 us -> 45.5 us (level)
  no operation moved by 1% of the time
where the time goes in v5:
time: 45.5 us; the launch traced here: 45.3 us
  Pallas kernels  43.6 us (96%)
  local copies, waits for them, and re-layouts  1.67 us (4%)
    pallas_call x1, Pallas kernels, per_device(): pl.pallas_call(functools.partial(kernel, ns, nd, slabs), out_shape=jax.Sh...  43.6 us
    unnamed x1, local copies, waits for them, and re-layouts  1.67 us

profile of v5, /device:TPU:6, one launch (start us, length us, event | category | flops | bytes accessed | tf_op | source)
XLA Modules:
  0.0 45.3 jit_solution(16029058015558628042)
XLA Ops:
  0.0 43.6 %shard_map.55 = bf16[128,1024]{1,0:T(8,128)(2,1)} custom-call(bf16[128,1024]{1,0:T(8,128)(2,1)} %bitcast.7, s32[128,256]{1,0:T(8,128)} %edges_hbm.1, s32[2,3]{1,0:T(2,128)} %picks.1, bf16[1024,1024]{1,0:T(8,128)(2,1)} %bitcast.4, bf16[1024,1024]{1,0:T(8,128)(2,1)} %bitcast.5), custom_call_target="tpu_custom_call" | custom-call | tf_op jit(solution)/shard_map/pallas_call | solution.py:658
  43.7 1.7 %copy.7 = bf16[1,128,1024]{2,1,0:T(8,128)(2,1)} copy(bf16[1,128,1024]{2,1,0:T(8,128)(2,1)} %bitcast.6) | data formatting | bytes 524288

commit v6 on v5

--- a/solution.py
+++ b/solution.py
@@ -553,10 +553,11 @@
                 relay(slots[c], ch, ())
 
         def use(ch, at_end=False):
-            for c in range(slabs):
+            mine = [last] if ch in near else range(slabs)
+            for c in mine:
                 rest(slots[c], ch)
             total = pre[:, cols(ch)]
-            for c in range(slabs):
+            for c in mine:
                 term = gather(c, slots[c], ch, pl.ds(c * block, (slabs - c) * block))
                 if c > 0:
                     term = jnp.concatenate([jnp.zeros((c * block, term.shape[1]), jnp.float32), term], axis=0)
@@ -571,6 +572,13 @@
         for c in range(slabs):
             relays(c, near)
         for c in range(slabs):
+            if c == last:
+                for ch in near:
+                    for j in range(last):
+                        rest(slots[j], ch)
+                        pre[j * block:, cols(ch)] += gather(
+                            j, slots[j], ch, pl.ds(j * block, (slabs - j) * block)
+                        )
             given_up(c)
             relays(c, distant)
         acc[...] += own_part(distant)

time: 45.5 us -> 45.4 us (level)
  no operation moved by 1% of the time
where the time goes in v6:
time: 45.4 us; the launch traced here: 45.3 us
  Pallas kernels  43.6 us (96%)
  local copies, waits for them, and re-layouts  1.67 us (4%)
    pallas_call x1, Pallas kernels, per_device(): pl.pallas_call(functools.partial(kernel, ns, nd, slabs), out_shape=jax.Sh...  43.6 us
    unnamed x1, local copies, waits for them, and re-layouts  1.67 us

profile of v6, /device:TPU:6, one launch (start us, length us, event | category | flops | bytes accessed | tf_op | source)
XLA Modules:
  0.0 45.3 jit_solution(2917597273701585834)
XLA Ops:
  0.0 43.6 %shard_map.55 = bf16[128,1024]{1,0:T(8,128)(2,1)} custom-call(bf16[128,1024]{1,0:T(8,128)(2,1)} %bitcast.7, s32[128,256]{1,0:T(8,128)} %edges_hbm.1, s32[2,3]{1,0:T(2,128)} %picks.1, bf16[1024,1024]{1,0:T(8,128)(2,1)} %bitcast.4, bf16[1024,1024]{1,0:T(8,128)(2,1)} %bitcast.5), custom_call_target="tpu_custom_call" | custom-call | tf_op jit(solution)/shard_map/pallas_call | solution.py:666
  43.6 1.7 %copy.7 = bf16[1,128,1024]{2,1,0:T(8,128)(2,1)} copy(bf16[1,128,1024]{2,1,0:T(8,128)(2,1)} %bitcast.6) | data formatting | bytes 524288
